TPU v7x, 256 devices: a whole 4x4x8 slice. The times are simulated.
256 devices in a mesh: wide: 32 (over z_hi, y, x), narrow: 8 (over z_lo, core).
Axes of the slice: x: 4, y: 4, z: 8 (z_hi: 2, z_lo: 4; z = z_hi * 4 + z_lo), core: 2. Of those that a mesh axis runs over, the one named last changes fastest.
Arguments:
- tile_pool: bfloat16 [32, 1024, 768], P('wide', 'narrow'), may hold values from -96 to 96
- batch_index: int32 [32, 2048], P('wide', 'narrow'), may hold values from 0 to 127
- pair_label: int32 [32, 2048], P('wide', 'narrow'), may hold values from 0 to 255, as said below
- w_first: bfloat16 [768, 2048], P('narrow'), may hold values from -0.375 to 0.375
- w_second: bfloat16 [2048, 2048], P('narrow'), may hold values from -0.375 to 0.375
- m_first: bfloat16 [32, 768, 2048], P('wide', 'narrow'), may hold values from -0.01275776 to 0.01275776
- m_second: bfloat16 [32, 2048, 2048], P('wide', 'narrow'), may hold values from -0.0078125 to 0.0078125
- v_first: bfloat16 [32, 768, 2048], P('wide', 'narrow'), may hold values from 0.0005086263 to 0.025431315
- v_second: bfloat16 [32, 2048, 2048], P('wide', 'narrow'), may hold values from 0.00019073486 to 0.009536743
- mom_first: bfloat16 [768, 2048], P('narrow'), may hold values from -0.1796875 to 0.1796875
- mom_second: bfloat16 [2048, 2048], P('narrow'), may hold values from -0.1796875 to 0.1796875
Outputs:
- new_first: bfloat16 [768, 2048], P('narrow')
- new_second: bfloat16 [2048, 2048], P('narrow')
- mom_out_first: bfloat16 [768, 2048], P('narrow')
- mom_out_second: bfloat16 [2048, 2048], P('narrow')
Inputs may be any that keep to these rules, and one draw needn't show every extreme that they name: `batch_index`: indices count within the pool of the same site and shard. `pair_label`: each row's partner is another row of the same site and shard, counted within that shard's 256 rows, and names the row back.
All inputs are finite; a program needn't handle non-finite values.
Results may differ from a plain program's by a relative error of at most 0.0075.
Values may be sent and summed in bfloat16 or wider, within the bound.
A program may use at most 128 MiB of HBM per device.

v0:
```python
import math
import jax
import jax.numpy as jnp
import numpy as np
from jax import lax
from jax.sharding import Mesh
from jax.sharding import PartitionSpec as P

PIX = 768
MID = 2048
OUT = 2048
logit_scale = 1.0 / 0.07
rate_inner = 0.2
weight_decay = 0.1
beta_first = 0.9
beta_second = 0.95
adam_eps = 1e-08
rate_outer = 0.7
momentum_coef = 0.9
WIDE = ("zh", "y", "x")
NARROW = ("zl", "c")


def adam_delta(grads, first_moment, second_moment, weights):
    moment_one = beta_first * first_moment.astype(jnp.float32) + (1.0 - beta_first) * grads
    moment_two = (
        beta_second * second_moment.astype(jnp.float32) + (1.0 - beta_second) * grads * grads
    )
    return rate_inner * (
        moment_one / (jnp.sqrt(moment_two) + adam_eps) + weight_decay * weights.astype(jnp.float32)
    )


def outer_update(delta, momentum, weights):
    velocity = momentum_coef * momentum.astype(jnp.float32) + delta
    updated = weights.astype(jnp.float32) - rate_outer * (delta + momentum_coef * velocity)
    return (updated.astype(jnp.bfloat16), velocity.astype(jnp.bfloat16))


def embed_gradient(embedded, partner):
    inverse = lax.rsqrt(jnp.sum(embedded * embedded, axis=1, keepdims=True) + OUT * 1e-06)
    unit_rows = embedded * inverse
    unit_half = unit_rows.astype(jnp.bfloat16)
    scores = logit_scale * jnp.dot(unit_half, unit_half.T, preferred_element_type=jnp.float32)
    positions = jnp.arange(embedded.shape[0], dtype=jnp.int32)
    diagonal = positions[:, None] == positions[None, :]
    scores = jnp.where(diagonal, -1e30, scores)
    highest = jnp.max(scores, axis=1, keepdims=True)
    powers = jnp.exp(scores - highest)
    softmax_rows = powers / jnp.sum(powers, axis=1, keepdims=True)
    target = (partner[:, None] == positions[None, :]).astype(jnp.float32)
    score_grad = softmax_rows - target
    paired = (score_grad + score_grad.T).astype(jnp.bfloat16)
    unit_grad = logit_scale * jnp.dot(paired, unit_half, preferred_element_type=jnp.float32)
    embed_grad = inverse * (
        unit_grad - unit_rows * jnp.sum(unit_rows * unit_grad, axis=1, keepdims=True)
    )
    return embed_grad.astype(jnp.bfloat16)


def wide_mean_update(delta, momentum, weights, axis):
    sites = lax.axis_size(WIDE)
    piece = delta.shape[axis] // sites
    got = lax.all_to_all(delta, WIDE, axis, axis, tiled=True)
    got = jnp.moveaxis(got, axis, 0).reshape((sites, piece) + (delta.shape[1 - axis],))
    mean = jnp.moveaxis(jnp.sum(got, axis=0), 0, axis) / sites
    start = lax.axis_index(WIDE) * piece
    mom_piece = lax.dynamic_slice_in_dim(momentum, start, piece, axis=axis)
    w_piece = lax.dynamic_slice_in_dim(weights, start, piece, axis=axis)
    new_piece, vel_piece = outer_update(mean, mom_piece, w_piece)
    both = jnp.stack([new_piece, vel_piece], axis=0)
    spread = jnp.broadcast_to(both[None], (sites,) + both.shape)
    back = lax.all_to_all(spread, WIDE, 0, 0, tiled=True)
    back = jnp.moveaxis(back, 0, 1 + axis)
    shape = list(delta.shape)
    back = back.reshape([2] + shape)
    return (back[0], back[1])


def shards(
    tile_pool,
    batch_index,
    pair_label,
    w_first,
    w_second,
    m_first,
    m_second,
    v_first,
    v_second,
    mom_first,
    mom_second,
):
    inputs = jnp.take(tile_pool[0], batch_index[0], axis=0)
    partner = pair_label[0]
    scale_one = 1.0 / math.sqrt(PIX)
    scale_two = 1.0 / math.sqrt(MID)
    hidden = (
        jnp.dot(
            inputs,
            lax.all_gather(w_first, NARROW, axis=0, tiled=True),
            preferred_element_type=jnp.float32,
        )
        * scale_one
    )
    active_full, gelu_back = jax.vjp(jax.nn.gelu, hidden)
    active = active_full.astype(jnp.bfloat16)
    second_whole = lax.all_gather(w_second, NARROW, axis=0, tiled=True)
    embedded = jnp.dot(active, second_whole, preferred_element_type=jnp.float32) * scale_two
    embed_half = embed_gradient(embedded, partner)
    active_grad = scale_two * jnp.dot(
        embed_half, second_whole.T, preferred_element_type=jnp.float32
    )
    hidden_half = gelu_back(active_grad)[0].astype(jnp.bfloat16)
    grad_first = lax.psum_scatter(
        (scale_one * jnp.dot(inputs.T, hidden_half, preferred_element_type=jnp.float32)).astype(
            jnp.bfloat16
        ),
        NARROW,
        scatter_dimension=0,
        tiled=True,
    ).astype(jnp.float32)
    delta_first = adam_delta(grad_first, m_first[0], v_first[0], w_first)
    new_first, vel_first = wide_mean_update(delta_first, mom_first, w_first, 1)
    term_second = (
        scale_two * jnp.dot(active.T, embed_half, preferred_element_type=jnp.float32)
    ).astype(jnp.bfloat16)
    halves = []
    cols = term_second.shape[1] // 2
    for h in range(2):
        part = slice(h * cols, (h + 1) * cols)
        grad_part = lax.psum_scatter(
            term_second[:, part], NARROW, scatter_dimension=0, tiled=True
        ).astype(jnp.float32)
        delta_part = adam_delta(
            grad_part, m_second[0][:, part], v_second[0][:, part], w_second[:, part]
        )
        halves.append(wide_mean_update(delta_part, mom_second[:, part], w_second[:, part], 0))
    new_second = jnp.concatenate([halves[0][0], halves[1][0]], axis=1)
    vel_second = jnp.concatenate([halves[0][1], halves[1][1]], axis=1)
    return (new_first, new_second, vel_first, vel_second)


def solution(mesh):
    zh, y, x = (2, 4, 4)
    devices = np.asarray(mesh.devices)
    wide, narrow = devices.shape
    sub = Mesh(devices.reshape(zh, y, x, narrow // 2, 2), WIDE + NARROW)
    site = P(WIDE, NARROW, None)
    rows = P(NARROW, None)
    return jax.shard_map(
        shards,
        mesh=sub,
        in_specs=(
            site,
            P(WIDE, NARROW),
            P(WIDE, NARROW),
            rows,
            rows,
            site,
            site,
            site,
            site,
            rows,
            rows,
        ),
        out_specs=(rows, rows, rows, rows),
        check_vma=False,
    )
```

profile of v0, /device:TPU:64, one launch (start us, length us, event | category | flops | bytes accessed | tf_op | source)
XLA Modules:
  0.0 523.8 jit_solution(6939493928089359772)
XLA Ops:
  9.4 1.2 gather_fusion
  10.6 42.6 %all-gather.3.cloned.1.call-done = bf16[768,2048]{1,0:T(8,128)(2,1)} async-done(((bf16[96,2048]{1,0:T(8,128)(2,1)}), bf16[768,2048]{1,0:T(8,128)(2,1)}) %all-gather.3.cloned.1.call-update) | async-done | bytes 3145744 | tf_op jit(solution)/shard_map/all_gather | solution.py:100
  53.2 4.4 convolution_multiply_fusion.1
  57.6 91.0 %all-gather.5.cloned.1.call-done = bf16[2048,2048]{1,0:T(8,128)(2,1)} async-done(((bf16[256,2048]{1,0:T(8,128)(2,1)}), bf16[2048,2048]{1,0:T(8,128)(2,1)}) %all-gather.5.cloned.1.call-update) | async-done | bytes 8388624 | tf_op jit(solution)/shard_map/all_gather | solution.py:107
  148.6 6.7 %multiply_reduce_fusion.1 = (f32[256]{0:T(256)S(1)}, f32[256,2048]{1,0:T(8,128)S(1)}) fusion(bf16[2048,2048]{1,0:T(8,128)(2,1)} %all-gather.5.cloned.1.call-done, f32[256,2048]{1,0:T(8,128)} %convolution_multiply_fusion.1), kind=kOutput, calls=%fused_computation.17 | convolution fusion | flops 2153774848 | bytes 12583936 | tf_op jit(solution)/shard_map/dot_general | solution.py:108
  157.1 1.5 multiply_convert_fusion.2
  158.6 10.1 %multiply_convert_fusion.1 = bf16[768,2048]{1,0:T(8,128)(2,1)} fusion(f32[256,2048]{1,0:T(8,128)} %convolution_multiply_fusion.1, bf16[256,2048]{1,0:T(8,128)(2,1)} %multiply_convert_fusion.2, bf16[2048,2048]{1,0:T(8,128)(2,1)} %all-gather.5.cloned.1.call-done, bf16[256,768]{1,0:T(8,128)(2,1)S(1)} %gather_fusion, pred[256]{0:T(512)(128)(4,1)S(1)} %compare_and_fusion), kind=kOutput, calls=%fused_computation.2 | convolution fusion | flops 2967142400 | bytes 15073536 | tf_op jit(solution)/shard_map/dot_general | solution.py:115
  169.1 1.3 copy-done.4
  170.7 3.0 multiply_convert_fusion
  173.6 3.8 fusion.77
  178.0 34.6 %reduce-scatter.4.cloned.1.call-done = bf16[96,2048]{1,0:T(8,128)(2,1)} async-done(((bf16[768,2048]{1,0:T(8,128)(2,1)}), bf16[96,2048]{1,0:T(8,128)(2,1)}) %reduce-scatter.4.cloned.1.call-update) | async-done | bytes 393232 | tf_op jit(solution)/shard_map/reduce_scatter | solution.py:114
  212.7 1.6 fusion.33
  214.3 1.3 copy.23
  215.6 9.9 %all-to-all-start = ((f32[96,32,64]{0,2,1:T(8,128)}), f32[96,32,64]{0,2,1:T(8,128)S(1)}, u32[]{:S(2)}, u32[]{:S(2)}) async-start(f32[96,32,64]{0,2,1:T(8,128)} %bitcast.8), calls=%async_computation.1 | async-start | bytes 2097152 | tf_op jit(solution)/shard_map/all_to_all | solution.py:64
  225.6 66.0 %reduce-scatter.6.cloned.1.call-done = bf16[256,1024]{1,0:T(8,128)(2,1)} async-done(((bf16[2048,1024]{1,0:T(8,128)(2,1)}), bf16[256,1024]{1,0:T(8,128)(2,1)}) %reduce-scatter.6.cloned.1.call-update) | async-done | bytes 524304 | tf_op jit(solution)/shard_map/reduce_scatter | solution.py:131
  291.5 54.9 %reduce-scatter.8.cloned.1.call-done = bf16[256,1024]{1,0:T(8,128)(2,1)} async-done(((bf16[2048,1024]{1,0:T(8,128)(2,1)}), bf16[256,1024]{1,0:T(8,128)(2,1)}) %reduce-scatter.8.cloned.1.call-update) | async-done | bytes 524304 | tf_op jit(solution)/shard_map/reduce_scatter | solution.py:131
  346.5 4.4 fusion.11
  351.9 42.4 %all_to_all.45 = f32[32,8,1024]{2,1,0:T(8,128)S(1)} all-to-all(f32[32,8,1024]{2,1,0:T(8,128)S(1)} %get-tuple-element.14), channel_id=1, replica_groups=mesh['zh'=2,'y'=4,'x'=4,'zl'=4,'c'=2] {'zh','y','x'}, dimensions={0} | all-to-all | bytes 2097152 | tf_op jit(solution)/shard_map/all_to_all | solution.py:64
  394.3 4.7 all-to-all-start.4
  400.5 1.4 constant_dynamic-slice_fusion.1
  401.9 1.4 copy.27
  403.4 1.3 bitcast_reduce_fusion
  406.0 20.2 %all-to-all-done.4 = f32[32,8,1024]{2,1,0:T(8,128)S(1)} async-done(((f32[32,8,1024]{2,1,0:T(8,128)}), f32[32,8,1024]{2,1,0:T(8,128)S(1)}, u32[]{:S(2)}, u32[]{:S(2)}) %all-to-all-start.4) | async-done | bytes 1048608 | tf_op jit(solution)/shard_map/all_to_all | solution.py:64
  426.2 2.0 broadcast_in_dim.23
  428.2 4.7 all-to-all-start.1
  436.2 21.0 %all-to-all-done.1 = bf16[32,2,96,64]{2,3,1,0:T(8,128)(2,1)} async-done(((bf16[32,2,96,64]{2,3,1,0:T(8,128)(2,1)}), bf16[32,2,96,64]{2,3,1,0:T(8,128)(2,1)}, u32[]{:S(2)}, u32[]{:S(2)}) %all-to-all-start.1) | async-done | bytes 786464 | tf_op jit(solution)/shard_map/all_to_all | solution.py:73
  457.1 1.1 broadcast_in_dim.25
  458.2 4.4 all-to-all-start.5
  462.7 22.9 %all-to-all-done.5 = bf16[32,2,8,1024]{3,2,1,0:T(8,128)(2,1)S(1)} async-done(((bf16[32,2,8,1024]{3,2,1,0:T(8,128)(2,1)}), bf16[32,2,8,1024]{3,2,1,0:T(8,128)(2,1)S(1)}, u32[]{:S(2)}, u32[]{:S(2)}) %all-to-all-start.5) | async-done | bytes 1048608 | tf_op jit(solution)/shard_map/all_to_all | solution.py:73
  486.7 4.9 all-to-all-start.3
  491.6 1.3 fusion.78
  494.9 20.2 %all-to-all-done.3 = bf16[32,2,8,1024]{3,2,1,0:T(8,128)(2,1)S(1)} async-done(((bf16[32,2,8,1024]{3,2,1,0:T(8,128)(2,1)}), bf16[32,2,8,1024]{3,2,1,0:T(8,128)(2,1)S(1)}, u32[]{:S(2)}, u32[]{:S(2)}) %all-to-all-start.3) | async-done | bytes 1048608 | tf_op jit(solution)/shard_map/all_to_all | solution.py:73
  (61 shorter events, 17.4 us)
Async XLA Ops:
  7.2 391.8 %copy-start = (bf16[96,2048]{1,0:T(8,128)(2,1)S(1)}, bf16[96,2048]{1,0:T(8,128)(2,1)}, u32[]{:S(2)}) copy-start(bf16[96,2048]{1,0:T(8,128)(2,1)} %param.20) | copy-start | bytes 1179652
  7.2 2.2 copy-start.1
  7.2 46.0 %all-gather.3.cloned.1.call-start = ((), (), s32[]{:S(2)}) async-start(), calls=%async_computation.9 | async-start | bytes 3538944 | tf_op jit(solution)/shard_map/all_gather | solution.py:100
  7.9 2.7 copy-start.10
  7.9 140.7 %all-gather.5.cloned.1.call-start = ((), (), s32[]{:S(2)}) async-start(), calls=%async_computation.10 | async-start | bytes 9437184 | tf_op jit(solution)/shard_map/all_gather | solution.py:107
  8.7 204.0 %reduce-scatter.4.cloned.1.call-start = ((), (), s32[]{:S(2)}) async-start(), calls=%async_computation.11 | async-start | bytes 3538944 | tf_op jit(solution)/shard_map/reduce_scatter | solution.py:114
  155.3 1.0 copy-start.11
  168.8 1.6 copy-start.4
  168.8 1.9 copy-start.7
  168.8 122.7 %reduce-scatter.6.cloned.1.call-start = ((), (), s32[]{:S(2)}) async-start(), calls=%async_computation.12 | async-start | bytes 4718592 | tf_op jit(solution)/shard_map/reduce_scatter | solution.py:131
  177.4 169.0 %reduce-scatter.8.cloned.1.call-start = ((), (), s32[]{:S(2)}) async-start(), calls=%async_computation.13 | async-start | bytes 4718592 | tf_op jit(solution)/shard_map/reduce_scatter | solution.py:131
  177.5 35.2 %copy-start.5 = (bf16[96,2048]{1,0:T(8,128)(2,1)S(1)}, bf16[96,2048]{1,0:T(8,128)(2,1)}, u32[]{:S(2)}) copy-start(bf16[96,2048]{1,0:T(8,128)(2,1)} %param.14) | copy-start | bytes 1179652
  177.5 35.2 %copy-start.8 = (bf16[1,96,2048]{2,1,0:T(8,128)(2,1)S(1)}, bf16[1,96,2048]{2,1,0:T(8,128)(2,1)}, u32[]{:S(2)}) copy-start(bf16[1,96,2048]{2,1,0:T(8,128)(2,1)} %param.18) | copy-start | bytes 1179652
  177.5 35.2 %copy-start.9 = (bf16[1,96,2048]{2,1,0:T(8,128)(2,1)S(1)}, bf16[1,96,2048]{2,1,0:T(8,128)(2,1)}, u32[]{:S(2)}) copy-start(bf16[1,96,2048]{2,1,0:T(8,128)(2,1)} %param.16) | copy-start | bytes 1179652
  214.3 132.1 %copy-start.2 = (bf16[256,2048]{1,0:T(8,128)(2,1)S(1)}, bf16[256,2048]{1,0:T(8,128)(2,1)}, u32[]{:S(2)}) copy-start(bf16[256,2048]{1,0:T(8,128)(2,1)} %param.15) | copy-start | bytes 3145732
  215.6 135.3 %all-to-all-start = ((f32[96,32,64]{0,2,1:T(8,128)}), f32[96,32,64]{0,2,1:T(8,128)S(1)}, u32[]{:S(2)}, u32[]{:S(2)}) async-start(f32[96,32,64]{0,2,1:T(8,128)} %bitcast.8), calls=%async_computation.1 | async-start | bytes 2097152 | tf_op jit(solution)/shard_map/all_to_all | solution.py:64
  350.9 1.0 copy-start.3
  394.3 32.0 %all-to-all-start.4 = ((f32[32,8,1024]{2,1,0:T(8,128)}), f32[32,8,1024]{2,1,0:T(8,128)S(1)}, u32[]{:S(2)}, u32[]{:S(2)}) async-start(f32[32,8,1024]{2,1,0:T(8,128)} %get-tuple-element.15), calls=%async_computation.7 | async-start | bytes 2097152 | tf_op jit(solution)/shard_map/all_to_all | solution.py:64
  428.2 28.9 %all-to-all-start.1 = ((bf16[32,2,96,64]{2,3,1,0:T(8,128)(2,1)}), bf16[32,2,96,64]{2,3,1,0:T(8,128)(2,1)}, u32[]{:S(2)}, u32[]{:S(2)}) async-start(bf16[32,2,96,64]{2,3,1,0:T(8,128)(2,1)} %broadcast_in_dim.23), calls=%async_computation.2 | async-start | bytes 2097152 | tf_op jit(solution)/shard_map/all_to_all | solution.py:73
  432.9 1.6 copy-start.6
  458.2 27.4 %all-to-all-start.5 = ((bf16[32,2,8,1024]{3,2,1,0:T(8,128)(2,1)}), bf16[32,2,8,1024]{3,2,1,0:T(8,128)(2,1)S(1)}, u32[]{:S(2)}, u32[]{:S(2)}) async-start(bf16[32,2,8,1024]{3,2,1,0:T(8,128)(2,1)} %broadcast_in_dim.25), calls=%async_computation.8 | async-start | bytes 2097152 | tf_op jit(solution)/shard_map/all_to_all | solution.py:73
  486.7 28.4 %all-to-all-start.3 = ((bf16[32,2,8,1024]{3,2,1,0:T(8,128)(2,1)}), bf16[32,2,8,1024]{3,2,1,0:T(8,128)(2,1)S(1)}, u32[]{:S(2)}, u32[]{:S(2)}) async-start(bf16[32,2,8,1024]{3,2,1,0:T(8,128)(2,1)} %broadcast_in_dim.24), calls=%async_computation.5 | async-start | bytes 2097152 | tf_op jit(solution)/shard_map/all_to_all | solution.py:73
Sparse Core Ops, SparseCore 0:
  9.8 43.3 all-gather.2
  55.0 93.5 all-gather.4
  168.9 43.6 reduce-scatter.3
  215.1 76.4 reduce-scatter.5
  293.9 52.4 reduce-scatter.7
where the time goes:
time: 525 us; the launch traced here: 524 us
  waiting for transfers between devices  375 us (71%)
  blocking collectives  42.4 us (8%)
  starting transfers between devices  29.1 us (6%)
  matrix products  25.5 us (5%)
  local copies, waits for them, and re-layouts  22.6 us (4%)
  other arithmetic  15 us (3%)
  between operations  14 us (3%)
    reduce_scatter x2, waiting for transfers between devices, shards(): lax.psum_scatter(term_second[:, part], NARROW, scatter_dimension=0, tiled...  121 us
    all_gather x1, waiting for transfers between devices, shards(): second_whole = lax.all_gather(w_second, NARROW, axis=0, tiled=True)  91 us
    all_to_all x3, waiting for transfers between devices, wide_mean_update(): back = lax.all_to_all(spread, WIDE, 0, 0, tiled=True)  64.1 us
    all_gather x1, waiting for transfers between devices, shards(): lax.all_gather(w_first, NARROW, axis=0, tiled=True)  42.6 us
    all_to_all x1, blocking collectives, wide_mean_update(): got = lax.all_to_all(delta, WIDE, axis, axis, tiled=True)  42.4 us
    reduce_scatter x1, waiting for transfers between devices, shards(): lax.psum_scatter((scale_one * jnp.dot(inputs.T, hidden_half, preferred_el...  34.6 us
    all_to_all x2, waiting for transfers between devices, wide_mean_update(): got = lax.all_to_all(delta, WIDE, axis, axis, tiled=True)  20.2 us
    all_to_all x2, starting transfers between devices, wide_mean_update(): got = lax.all_to_all(delta, WIDE, axis, axis, tiled=True)  14.6 us
  transfers between devices with their start and end apart: 10, of which 9 were waited for; matrix products, arithmetic and copies ran while one was open for 6% of the time, Pallas kernels for 0%

commit v1 on v0

--- a/solution.py
+++ b/solution.py
@@ -104,7 +104,13 @@
     )
     active_full, gelu_back = jax.vjp(jax.nn.gelu, hidden)
     active = active_full.astype(jnp.bfloat16)
-    second_whole = lax.all_gather(w_second, NARROW, axis=0, tiled=True)
+    pipes_find = lambda values, group_axis: jnp.concatenate(
+        lax.all_to_all(
+            jnp.stack([values] * lax.axis_size(group_axis)), group_axis, split_axis=0, concat_axis=0
+        ),
+        axis=0,
+    )
+    second_whole = pipes_find(w_second, NARROW)
     embedded = jnp.dot(active, second_whole, preferred_element_type=jnp.float32) * scale_two
     embed_half = embed_gradient(embedded, partner)
     active_grad = scale_two * jnp.dot(

time: 525 us -> 609 us (1.16)
  waiting for transfers between devices: 375 us -> 448 us
  starting transfers between devices: 29.1 us -> 35.4 us
    all_to_all x0 -> x1, waiting for transfers between devices: none -> 92.3 us  [shards(): lax.all_to_all(jnp.stack([values] * lax.axis_size(group_axis)), group_axi...]
    all_gather x1 -> x0, waiting for transfers between devices: 91 us -> none  [shards(): second_whole = lax.all_gather(w_second, NARROW, axis=0, tiled=True)]
    all_gather x1, waiting for transfers between devices: 42.6 us -> 111 us  [shards(): lax.all_gather(w_first, NARROW, axis=0, tiled=True)]
    all_to_all x0 -> x1, starting transfers between devices: none -> 6.34 us  [shards(): lax.all_to_all(jnp.stack([values] * lax.axis_size(group_axis)), group_axi...]
  transfers between devices with their start and end apart: 10 -> 10, of which waited for: 9 -> 9; matrix products, arithmetic and copies ran while one was open for 6% -> 5% of each run, Pallas kernels for 0% -> 0%
where the time goes in v1:
time: 609 us; the launch traced here: 607 us
  waiting for transfers between devices  448 us (74%)
  blocking collectives  42.4 us (7%)
  starting transfers between devices  35.4 us (6%)
  local copies, waits for them, and re-layouts  28.3 us (5%)
  matrix products  25.4 us (4%)
  other arithmetic  14.3 us (2%)
  between operations  14 us (2%)
    reduce_scatter x2, waiting for transfers between devices, shards(): lax.psum_scatter(term_second[:, part], NARROW, scatter_dimension=0, tiled...  121 us
    all_gather x1, waiting for transfers between devices, shards(): lax.all_gather(w_first, NARROW, axis=0, tiled=True)  111 us
    all_to_all x1, waiting for transfers between devices, shards(): lax.all_to_all(jnp.stack([values] * lax.axis_size(group_axis)), group_axi...  92.3 us
    all_to_all x3, waiting for transfers between devices, wide_mean_update(): back = lax.all_to_all(spread, WIDE, 0, 0, tiled=True)  64.1 us
    all_to_all x1, blocking collectives, wide_mean_update(): got = lax.all_to_all(delta, WIDE, axis, axis, tiled=True)  42.4 us
    reduce_scatter x1, waiting for transfers between devices, shards(): lax.psum_scatter((scale_one * jnp.dot(inputs.T, hidden_half, preferred_el...  37.6 us
    all_to_all x2, waiting for transfers between devices, wide_mean_update(): got = lax.all_to_all(delta, WIDE, axis, axis, tiled=True)  20.4 us
    all_to_all x2, starting transfers between devices, wide_mean_update(): got = lax.all_to_all(delta, WIDE, axis, axis, tiled=True)  14.8 us
  transfers between devices with their start and end apart: 10, of which 9 were waited for; matrix products, arithmetic and copies ran while one was open for 5% of the time, Pallas kernels for 0%

profile of v1, /device:TPU:64, one launch (start us, length us, event | category | flops | bytes accessed | tf_op | source)
XLA Modules:
  0.0 607.5 jit_solution(4357781904285476638)
XLA Ops:
  7.2 5.6 stack.38
  12.8 6.3 %all-to-all-start = ((bf16[8,256,2048]{2,1,0:T(8,128)(2,1)}), bf16[8,256,2048]{2,1,0:T(8,128)(2,1)}, u32[]{:S(2)}, u32[]{:S(2)}) async-start(bf16[8,256,2048]{2,1,0:T(8,128)(2,1)} %stack.38), calls=%async_computation | async-start | bytes 16777216 | tf_op jit(solution)/shard_map/all_to_all | solution.py:108
  21.2 111.3 %all-gather.2.cloned.1.call-done = bf16[768,2048]{1,0:T(8,128)(2,1)} async-done(((bf16[96,2048]{1,0:T(8,128)(2,1)}), bf16[768,2048]{1,0:T(8,128)(2,1)}) %all-gather.2.cloned.1.call-update) | async-done | bytes 3145744 | tf_op jit(solution)/shard_map/all_gather | solution.py:100
  132.5 4.3 convolution_multiply_fusion.1
  136.9 92.3 %all-to-all-done = bf16[8,256,2048]{2,1,0:T(8,128)(2,1)} async-done(((bf16[8,256,2048]{2,1,0:T(8,128)(2,1)}), bf16[8,256,2048]{2,1,0:T(8,128)(2,1)}, u32[]{:S(2)}, u32[]{:S(2)}) %all-to-all-start) | async-done | bytes 8388640 | tf_op jit(solution)/shard_map/all_to_all | solution.py:108
  229.2 6.7 %multiply_reduce_fusion.1 = (f32[256]{0:T(256)S(1)}, f32[256,2048]{1,0:T(8,128)S(1)}) fusion(bf16[2048,2048]{1,0:T(8,128)(2,1)} %bitcast.5, f32[256,2048]{1,0:T(8,128)} %convolution_multiply_fusion.1), kind=kOutput, calls=%fused_computation.17 | convolution fusion | flops 2153774848 | bytes 12583936 | tf_op jit(solution)/shard_map/dot_general | solution.py:114
  237.7 1.5 multiply_convert_fusion.2
  239.2 10.2 %multiply_convert_fusion.1 = bf16[768,2048]{1,0:T(8,128)(2,1)} fusion(f32[256,2048]{1,0:T(8,128)} %convolution_multiply_fusion.1, bf16[256,2048]{1,0:T(8,128)(2,1)} %multiply_convert_fusion.2, bf16[2048,2048]{1,0:T(8,128)(2,1)} %bitcast.5, bf16[256,768]{1,0:T(8,128)(2,1)S(1)} %gather_fusion, pred[256]{0:T(512)(128)(4,1)S(1)} %compare_and_fusion), kind=kOutput, calls=%fused_computation.2 | convolution fusion | flops 2967142400 | bytes 15073536 | tf_op jit(solution)/shard_map/dot_general | solution.py:121
  249.6 1.3 copy-done.4
  251.2 3.0 multiply_convert_fusion
  254.2 3.8 fusion.77
  258.6 37.6 %reduce-scatter.4.cloned.1.call-done = bf16[96,2048]{1,0:T(8,128)(2,1)} async-done(((bf16[768,2048]{1,0:T(8,128)(2,1)}), bf16[96,2048]{1,0:T(8,128)(2,1)}) %reduce-scatter.4.cloned.1.call-update) | async-done | bytes 393232 | tf_op jit(solution)/shard_map/reduce_scatter | solution.py:120
  296.2 1.6 fusion.33
  297.8 1.3 copy.23
  299.2 10.0 %all-to-all-start.1 = ((f32[96,32,64]{0,2,1:T(8,128)}), f32[96,32,64]{0,2,1:T(8,128)S(1)}, u32[]{:S(2)}, u32[]{:S(2)}) async-start(f32[96,32,64]{0,2,1:T(8,128)} %bitcast.9), calls=%async_computation.2 | async-start | bytes 2097152 | tf_op jit(solution)/shard_map/all_to_all | solution.py:64
  309.1 65.9 %reduce-scatter.6.cloned.1.call-done = bf16[256,1024]{1,0:T(8,128)(2,1)} async-done(((bf16[2048,1024]{1,0:T(8,128)(2,1)}), bf16[256,1024]{1,0:T(8,128)(2,1)}) %reduce-scatter.6.cloned.1.call-update) | async-done | bytes 524304 | tf_op jit(solution)/shard_map/reduce_scatter | solution.py:137
  375.1 54.8 %reduce-scatter.8.cloned.1.call-done = bf16[256,1024]{1,0:T(8,128)(2,1)} async-done(((bf16[2048,1024]{1,0:T(8,128)(2,1)}), bf16[256,1024]{1,0:T(8,128)(2,1)}) %reduce-scatter.8.cloned.1.call-update) | async-done | bytes 524304 | tf_op jit(solution)/shard_map/reduce_scatter | solution.py:137
  429.9 4.4 fusion.11
  435.3 42.4 %all_to_all.50 = f32[32,8,1024]{2,1,0:T(8,128)S(1)} all-to-all(f32[32,8,1024]{2,1,0:T(8,128)S(1)} %get-tuple-element.14), channel_id=1, replica_groups=mesh['zh'=2,'y'=4,'x'=4,'zl'=4,'c'=2] {'zh','y','x'}, dimensions={0} | all-to-all | bytes 2097152 | tf_op jit(solution)/shard_map/all_to_all | solution.py:64
  477.7 4.8 all-to-all-start.5
  484.0 1.4 constant_dynamic-slice_fusion.1
  485.4 1.4 copy.27
  486.9 1.3 bitcast_reduce_fusion
  489.6 20.4 %all-to-all-done.5 = f32[32,8,1024]{2,1,0:T(8,128)S(1)} async-done(((f32[32,8,1024]{2,1,0:T(8,128)}), f32[32,8,1024]{2,1,0:T(8,128)S(1)}, u32[]{:S(2)}, u32[]{:S(2)}) %all-to-all-start.5) | async-done | bytes 1048608 | tf_op jit(solution)/shard_map/all_to_all | solution.py:64
  509.9 2.0 broadcast_in_dim.23
  511.9 4.7 all-to-all-start.2
  519.8 21.0 %all-to-all-done.2 = bf16[32,2,96,64]{2,3,1,0:T(8,128)(2,1)} async-done(((bf16[32,2,96,64]{2,3,1,0:T(8,128)(2,1)}), bf16[32,2,96,64]{2,3,1,0:T(8,128)(2,1)}, u32[]{:S(2)}, u32[]{:S(2)}) %all-to-all-start.2) | async-done | bytes 786464 | tf_op jit(solution)/shard_map/all_to_all | solution.py:73
  541.9 4.4 all-to-all-start.6
  546.4 22.9 %all-to-all-done.6 = bf16[32,2,8,1024]{3,2,1,0:T(8,128)(2,1)S(1)} async-done(((bf16[32,2,8,1024]{3,2,1,0:T(8,128)(2,1)}), bf16[32,2,8,1024]{3,2,1,0:T(8,128)(2,1)S(1)}, u32[]{:S(2)}, u32[]{:S(2)}) %all-to-all-start.6) | async-done | bytes 1048608 | tf_op jit(solution)/shard_map/all_to_all | solution.py:73
  570.3 4.9 all-to-all-start.4
  575.3 1.3 fusion.78
  578.6 20.2 %all-to-all-done.4 = bf16[32,2,8,1024]{3,2,1,0:T(8,128)(2,1)S(1)} async-done(((bf16[32,2,8,1024]{3,2,1,0:T(8,128)(2,1)}), bf16[32,2,8,1024]{3,2,1,0:T(8,128)(2,1)S(1)}, u32[]{:S(2)}, u32[]{:S(2)}) %all-to-all-start.4) | async-done | bytes 1048608 | tf_op jit(solution)/shard_map/all_to_all | solution.py:73
  (61 shorter events, 18.4 us)
Async XLA Ops:
  7.2 475.3 %copy-start = (bf16[96,2048]{1,0:T(8,128)(2,1)S(1)}, bf16[96,2048]{1,0:T(8,128)(2,1)}, u32[]{:S(2)}) copy-start(bf16[96,2048]{1,0:T(8,128)(2,1)} %param.20) | copy-start | bytes 1179652
  12.8 7.1 %copy-start.10 = (s32[1,256]{1,0:T(1,128)S(1)}, s32[1,256]{1,0:T(1,128)}, u32[]{:S(2)}) copy-start(s32[1,256]{1,0:T(1,128)} %param.12) | copy-start | bytes 3076
  12.8 216.4 %all-to-all-start = ((bf16[8,256,2048]{2,1,0:T(8,128)(2,1)}), bf16[8,256,2048]{2,1,0:T(8,128)(2,1)}, u32[]{:S(2)}, u32[]{:S(2)}) async-start(bf16[8,256,2048]{2,1,0:T(8,128)(2,1)} %stack.38), calls=%async_computation | async-start | bytes 16777216 | tf_op jit(solution)/shard_map/all_to_all | solution.py:108
  19.1 0.9 copy-start.1
  19.1 113.4 %all-gather.2.cloned.1.call-start = ((), (), s32[]{:S(2)}) async-start(), calls=%async_computation.10 | async-start | bytes 3538944 | tf_op jit(solution)/shard_map/all_gather | solution.py:100
  19.8 276.4 %reduce-scatter.4.cloned.1.call-start = ((), (), s32[]{:S(2)}) async-start(), calls=%async_computation.11 | async-start | bytes 3538944 | tf_op jit(solution)/shard_map/reduce_scatter | solution.py:120
  235.9 1.0 copy-start.11
  249.4 1.6 copy-start.4
  249.4 1.9 copy-start.7
  249.4 125.7 %reduce-scatter.6.cloned.1.call-start = ((), (), s32[]{:S(2)}) async-start(), calls=%async_computation.12 | async-start | bytes 4718592 | tf_op jit(solution)/shard_map/reduce_scatter | solution.py:137
  258.0 171.9 %reduce-scatter.8.cloned.1.call-start = ((), (), s32[]{:S(2)}) async-start(), calls=%async_computation.13 | async-start | bytes 4718592 | tf_op jit(solution)/shard_map/reduce_scatter | solution.py:137
  258.1 38.2 %copy-start.5 = (bf16[96,2048]{1,0:T(8,128)(2,1)S(1)}, bf16[96,2048]{1,0:T(8,128)(2,1)}, u32[]{:S(2)}) copy-start(bf16[96,2048]{1,0:T(8,128)(2,1)} %param.14) | copy-start | bytes 1179652
  258.1 38.1 %copy-start.8 = (bf16[1,96,2048]{2,1,0:T(8,128)(2,1)S(1)}, bf16[1,96,2048]{2,1,0:T(8,128)(2,1)}, u32[]{:S(2)}) copy-start(bf16[1,96,2048]{2,1,0:T(8,128)(2,1)} %param.18) | copy-start | bytes 1179652
  258.1 38.1 %copy-start.9 = (bf16[1,96,2048]{2,1,0:T(8,128)(2,1)S(1)}, bf16[1,96,2048]{2,1,0:T(8,128)(2,1)}, u32[]{:S(2)}) copy-start(bf16[1,96,2048]{2,1,0:T(8,128)(2,1)} %param.16) | copy-start | bytes 1179652
  297.8 132.1 %copy-start.2 = (bf16[256,2048]{1,0:T(8,128)(2,1)S(1)}, bf16[256,2048]{1,0:T(8,128)(2,1)}, u32[]{:S(2)}) copy-start(bf16[256,2048]{1,0:T(8,128)(2,1)} %param.15) | copy-start | bytes 3145732
  299.2 135.2 %all-to-all-start.1 = ((f32[96,32,64]{0,2,1:T(8,128)}), f32[96,32,64]{0,2,1:T(8,128)S(1)}, u32[]{:S(2)}, u32[]{:S(2)}) async-start(f32[96,32,64]{0,2,1:T(8,128)} %bitcast.9), calls=%async_computation.2 | async-start | bytes 2097152 | tf_op jit(solution)/shard_map/all_to_all | solution.py:64
  434.3 1.0 copy-start.3
  477.7 32.2 %all-to-all-start.5 = ((f32[32,8,1024]{2,1,0:T(8,128)}), f32[32,8,1024]{2,1,0:T(8,128)S(1)}, u32[]{:S(2)}, u32[]{:S(2)}) async-start(f32[32,8,1024]{2,1,0:T(8,128)} %get-tuple-element.15), calls=%async_computation.8 | async-start | bytes 2097152 | tf_op jit(solution)/shard_map/all_to_all | solution.py:64
  511.9 28.9 %all-to-all-start.2 = ((bf16[32,2,96,64]{2,3,1,0:T(8,128)(2,1)}), bf16[32,2,96,64]{2,3,1,0:T(8,128)(2,1)}, u32[]{:S(2)}, u32[]{:S(2)}) async-start(bf16[32,2,96,64]{2,3,1,0:T(8,128)(2,1)} %broadcast_in_dim.23), calls=%async_computation.3 | async-start | bytes 2097152 | tf_op jit(solution)/shard_map/all_to_all | solution.py:73
  516.6 1.6 copy-start.6
  541.9 27.3 %all-to-all-start.6 = ((bf16[32,2,8,1024]{3,2,1,0:T(8,128)(2,1)}), bf16[32,2,8,1024]{3,2,1,0:T(8,128)(2,1)S(1)}, u32[]{:S(2)}, u32[]{:S(2)}) async-start(bf16[32,2,8,1024]{3,2,1,0:T(8,128)(2,1)} %broadcast_in_dim.25), calls=%async_computation.9 | async-start | bytes 2097152 | tf_op jit(solution)/shard_map/all_to_all | solution.py:73
  570.3 28.4 %all-to-all-start.4 = ((bf16[32,2,8,1024]{3,2,1,0:T(8,128)(2,1)}), bf16[32,2,8,1024]{3,2,1,0:T(8,128)(2,1)S(1)}, u32[]{:S(2)}, u32[]{:S(2)}) async-start(bf16[32,2,8,1024]{3,2,1,0:T(8,128)(2,1)} %broadcast_in_dim.24), calls=%async_computation.6 | async-start | bytes 2097152 | tf_op jit(solution)/shard_map/all_to_all | solution.py:73
Sparse Core Ops, SparseCore 0:
  21.7 110.8 all-gather.1
  249.5 46.6 reduce-scatter.3
  298.8 76.2 reduce-scatter.5
  377.5 52.3 reduce-scatter.7
